TPU v7x, 128 devices: a whole 4x4x4 slice. The times are simulated.
128 devices in a mesh: dp: 16 (over z, y), mp: 8 (over x, core).
Axes of the slice: x: 4, y: 4, z: 4, core: 2. Of those that a mesh axis runs over, the one named last changes fastest.
Arguments:
- residual: bfloat16 [2048, 4096], P('dp', 'mp'), may hold values from -18 to 18
- queries: bfloat16 [2048, 4096], P('dp', 'mp'), may hold values from -20 to 20
- new_keys: bfloat16 [2048, 1024], P('dp', 'mp'), may hold values from -6 to 6
- new_values: bfloat16 [2048, 1024], P('dp', 'mp'), may hold values from -6 to 6
- cache_keys: bfloat16 [2048, 16, 1024], P('dp', None, 'mp'), may hold values from -6 to 6
- cache_values: bfloat16 [2048, 16, 1024], P('dp', None, 'mp'), may hold values from -6 to 6
- cache_len: int32 [1024], replicated, may hold values from 1 to 128, 16384 in all
- page_order: int32 [2048], replicated, may hold values from 0 to 2047, each once
- out_proj: bfloat16 [4096, 4096], P('mp'), may hold values from -0.09375 to 0.09375
- attn_gain: float32 [4096], replicated, may hold values from 0.25 to 1.75
- routes: int32 [2048, 2], P('dp'), may hold values from 0 to 7, all different within a row; in each aligned block of 128 rows (0 to 127, 128 to 255, ...) at most 48 rows name the same one
- route_weight: float32 [2048, 2], P('dp'), may hold values from 0.1 to 1
- gate_proj: bfloat16 [4096, 98304], P(None, ('dp', 'mp')), may hold values from -0.09375 to 0.09375
- up_proj: bfloat16 [4096, 98304], P(None, ('dp', 'mp')), may hold values from -0.09375 to 0.09375
- down_proj: bfloat16 [98304, 4096], P(('dp', 'mp')), may hold values from -0.0546875 to 0.0546875
- final_gain: float32 [4096], P('mp'), may hold values from 0.25 to 1.75
Outputs:
- layer_out: bfloat16 [2048, 4096], P('dp', 'mp')
Inputs may be any that keep to these rules, and one draw needn't show every extreme that they name: `routes`: in each aligned block of 128 rows (the rows of one dp group) no expert is named by more than 48 rows, a bound that some block reaches; a row's two experts differ. `cache_len`: the lengths sum to 16384, and the longest is exactly 128. `page_order`: each page number appears once; pages past the last request's are unused.
All inputs are finite; a program needn't handle non-finite values.
Results may differ from a plain program's by a relative error of at most 0.008.
Values may be sent and summed in bfloat16 or wider, within the bound.
A program may use at most 128 MiB of HBM per device.

v0:
```python
import jax
import jax.numpy as jnp
from jax import lax
from jax.sharding import PartitionSpec as P

D = 4096
HQ = 32
KVH = 8
HD = 128
E = 8
PAGE = 16
DEC = 64
PRE = 64
C = 48
neg_big = -1e30
eps_norm = 1e-05


def page_owner(page_ids, page_order, cache_len):
    page_count = (cache_len + PAGE - 1) // PAGE
    page_ends = jnp.cumsum(page_count)
    page_first = page_ends - page_count
    pool_iota = lax.broadcasted_iota(jnp.int32, (1, page_order.shape[0]), 1)
    order_pos = jnp.sum(jnp.where(page_order[None, :] == page_ids[:, None], pool_iota, 0), axis=1)
    owners = jnp.sum((page_ends[None, :] <= order_pos[:, None]).astype(jnp.int32), axis=1)
    request_iota = lax.broadcasted_iota(jnp.int32, (1, cache_len.shape[0]), 1)
    chosen = request_iota == owners[:, None]
    first_own = jnp.sum(jnp.where(chosen, page_first[None, :], 0), axis=1)
    length_own = jnp.sum(jnp.where(chosen, cache_len[None, :], 0), axis=1)
    offsets = lax.broadcasted_iota(jnp.int32, (1, PAGE), 1)
    key_pos = (order_pos - first_own)[:, None] * PAGE + offsets
    return (owners, key_pos < length_own[:, None])


def page_partials(page_queries, key_pages, value_pages, key_ok, scale):
    scores = (
        jnp.einsum("pkgh,pokh->pkgo", page_queries, key_pages, preferred_element_type=jnp.float32)
        * scale
    )
    wide_mask = key_ok[:, None, None, :]
    masked = jnp.where(wide_mask, scores, neg_big)
    maxima = jnp.max(masked, axis=3)
    weights = jnp.where(wide_mask, jnp.exp(masked - maxima[..., None]), 0.0)
    totals = jnp.sum(weights, axis=3)
    weighted = jnp.einsum(
        "pkgo,pokh->pkgh",
        weights,
        value_pages.astype(jnp.float32),
        precision=lax.Precision.HIGHEST,
        preferred_element_type=jnp.float32,
    )
    return (maxima, totals, weighted)


def fold_pages(maxima, totals, weighted, owned, local_owner):
    top_score = jnp.max(jnp.where(owned[:, :, None, None], maxima[:, None], neg_big), axis=0)
    page_top = top_score[local_owner]
    factors = jnp.exp(maxima - page_top)
    owned_float = owned.astype(jnp.float32)
    sums = jnp.einsum("pr,pkg->rkg", owned_float, totals * factors, precision=lax.Precision.HIGHEST)
    values = jnp.einsum(
        "pr,pkgh->rkgh", owned_float, weighted * factors[..., None], precision=lax.Precision.HIGHEST
    )
    return (top_score, sums, values)


def local(
    residual,
    queries,
    new_keys,
    new_values,
    cache_keys,
    cache_values,
    cache_len,
    page_order,
    out_proj,
    attn_gain,
    routes,
    route_weight,
    gate_proj,
    up_proj,
    down_proj,
    final_gain,
):
    dp_count = lax.axis_size("dp")
    dp_index = lax.axis_index("dp")
    mp_index = lax.axis_index("mp")
    scale = HD ** (-0.5)
    kv_local = new_keys.shape[1] // HD
    group_size = HQ // KVH
    width_local = residual.shape[1]
    pool_local = cache_keys.shape[0]
    request_total = cache_len.shape[0]
    query_heads = queries[:DEC].reshape(DEC, kv_local, group_size, HD)
    gathered = lax.all_gather(queries[:DEC], "dp", axis=0, tiled=True)
    gathered_heads = gathered.reshape(request_total, kv_local, group_size, HD)
    page_ids = dp_index * pool_local + lax.broadcasted_iota(jnp.int32, (pool_local,), 0)
    owners, key_ok = page_owner(page_ids, page_order, cache_len)
    live = owners < request_total
    local_owner = jnp.minimum(owners, request_total - 1)
    key_ok = key_ok & live[:, None]
    key_pages = cache_keys.reshape(pool_local, PAGE, kv_local, HD)
    value_pages = cache_values.reshape(pool_local, PAGE, kv_local, HD)
    page_queries = gathered_heads[local_owner]
    maxima, totals, weighted = page_partials(page_queries, key_pages, value_pages, key_ok, scale)
    owned = (local_owner[:, None] == lax.broadcasted_iota(jnp.int32, (1, request_total), 1)) & live[
        :, None
    ]
    maxima, totals, weighted = fold_pages(maxima, totals, weighted, owned, local_owner)
    maxima = maxima.reshape(dp_count, DEC, kv_local, group_size)
    totals = totals.reshape(dp_count, DEC, kv_local, group_size)
    weighted = weighted.reshape(dp_count, DEC, kv_local, group_size, HD)
    maxima, totals, weighted = (
        lax.all_to_all(maxima, "dp", split_axis=0, concat_axis=0, tiled=True),
        lax.all_to_all(totals, "dp", split_axis=0, concat_axis=0, tiled=True),
        lax.all_to_all(weighted, "dp", split_axis=0, concat_axis=0, tiled=True),
    )
    top_cache = jnp.max(maxima, axis=0)
    factors = jnp.exp(maxima - top_cache[None])
    cache_state = (
        top_cache,
        jnp.sum(totals * factors, axis=0),
        jnp.sum(weighted * factors[..., None], axis=0),
    )
    self_keys = new_keys[:DEC].reshape(DEC, kv_local, HD)
    self_values = new_values[:DEC].reshape(DEC, kv_local, HD).astype(jnp.float32)
    self_score = (
        jnp.einsum("rkgh,rkh->rkg", query_heads, self_keys, preferred_element_type=jnp.float32)
        * scale
    )
    cache_top, cache_total, cache_sum = cache_state
    top_score = jnp.maximum(cache_top, self_score)
    cache_factor = jnp.exp(cache_top - top_score)
    self_factor = jnp.exp(self_score - top_score)
    numerator = (
        cache_sum * cache_factor[..., None] + self_factor[..., None] * self_values[:, :, None, :]
    )
    denominator = cache_total * cache_factor + self_factor
    decode_out = (numerator / denominator[..., None]).astype(jnp.bfloat16).reshape(DEC, -1)
    prompt_q = queries[DEC:].reshape(PRE, kv_local, group_size, HD)
    prompt_k = new_keys[DEC:].reshape(PRE, kv_local, HD)
    prompt_v = new_values[DEC:].reshape(PRE, kv_local, HD).astype(jnp.float32)
    prompt_scores = (
        jnp.einsum("qkgh,tkh->kgqt", prompt_q, prompt_k, preferred_element_type=jnp.float32) * scale
    )
    causal = lax.broadcasted_iota(jnp.int32, (PRE, PRE), 0) >= lax.broadcasted_iota(
        jnp.int32, (PRE, PRE), 1
    )
    masked = jnp.where(causal, prompt_scores, neg_big)
    top_prompt = jnp.max(masked, axis=-1, keepdims=True)
    prompt_weights = jnp.where(causal, jnp.exp(masked - top_prompt), 0.0)
    prompt_num = jnp.einsum(
        "kgqt,tkh->qkgh",
        prompt_weights,
        prompt_v,
        precision=lax.Precision.HIGHEST,
        preferred_element_type=jnp.float32,
    )
    prompt_den = jnp.sum(prompt_weights, axis=-1).transpose(2, 0, 1)
    prompt_out = (prompt_num / prompt_den[..., None]).astype(jnp.bfloat16).reshape(PRE, -1)
    attn = jnp.concatenate([decode_out, prompt_out], axis=0)
    head_terms = jnp.dot(attn, out_proj, preferred_element_type=jnp.float32)
    column_start = mp_index * width_local
    own_columns = lax.dynamic_slice_in_dim(
        head_terms, column_start, width_local, 1
    ) + residual.astype(jnp.float32)
    head_terms = lax.dynamic_update_slice_in_dim(head_terms, own_columns, column_start, 1)
    hidden_full = lax.psum(head_terms, "mp")
    normed = (
        hidden_full
        * lax.rsqrt(jnp.mean(hidden_full * hidden_full, axis=1, keepdims=True) + eps_norm)
        * attn_gain[None, :]
    ).astype(jnp.bfloat16)
    hidden_cols = lax.dynamic_slice_in_dim(hidden_full, column_start, width_local, 1)
    tok_rows = residual.shape[0]
    pairs = routes.reshape(-1)
    onehot = (pairs[:, None] == lax.broadcasted_iota(jnp.int32, (1, E), 1)).astype(jnp.int32)
    slots = jnp.sum((jnp.cumsum(onehot, axis=0) - onehot) * onehot, axis=1)
    target = pairs * C + slots
    cells = lax.broadcasted_iota(jnp.int32, (1, E * C), 1)
    hits = (target[:, None] == cells).reshape(tok_rows, 2, E * C)
    dispatch = jnp.any(hits, axis=1).astype(jnp.bfloat16)
    combine = jnp.sum(jnp.where(hits, route_weight[:, :, None], 0.0), axis=1)
    buffer = lax.dot_general(
        dispatch, normed, (((0,), (0,)), ((), ())), preferred_element_type=jnp.float32
    ).astype(jnp.bfloat16)
    send = jnp.repeat(buffer.reshape(E, C, normed.shape[1]), dp_count // E, axis=0)
    arrived = lax.all_to_all(send, "dp", split_axis=0, concat_axis=0, tiled=True)
    gate_sum = jnp.einsum("scd,df->scf", arrived, gate_proj, preferred_element_type=jnp.float32)
    up_sum = jnp.einsum("scd,df->scf", arrived, up_proj, preferred_element_type=jnp.float32)
    hidden = (jax.nn.silu(gate_sum) * up_sum).astype(jnp.bfloat16)
    down_part = jnp.einsum("scf,fd->scd", hidden, down_proj, preferred_element_type=jnp.float32)
    shares = lax.psum_scatter(
        down_part.astype(jnp.bfloat16), "mp", scatter_dimension=2, tiled=True
    ).astype(jnp.float32)
    returned = lax.all_to_all(shares, "dp", split_axis=0, concat_axis=0, tiled=True)
    back = (
        returned.reshape(E, dp_count // E, C, width_local).sum(axis=1).reshape(E * C, width_local)
    )
    moe_rows = jnp.dot(
        combine, back, precision=lax.Precision.HIGHEST, preferred_element_type=jnp.float32
    )
    mixed = hidden_cols + moe_rows
    square_last = lax.psum(jnp.sum(mixed * mixed, axis=1), "mp")
    scaled = mixed * lax.rsqrt(square_last / D + eps_norm)[:, None] * final_gain[None, :]
    return scaled.astype(jnp.bfloat16)


def solution(mesh):
    return jax.shard_map(
        local,
        mesh=mesh,
        in_specs=(
            P("dp", "mp"),
            P("dp", "mp"),
            P("dp", "mp"),
            P("dp", "mp"),
            P("dp", None, "mp"),
            P("dp", None, "mp"),
            P(),
            P(),
            P("mp", None),
            P(),
            P("dp", None),
            P("dp", None),
            P(None, ("dp", "mp")),
            P(None, ("dp", "mp")),
            P(("dp", "mp"), None),
            P("mp"),
        ),
        out_specs=P("dp", "mp"),
        check_vma=False,
    )
```

profile of v0, /device:TPU:0, one launch (start us, length us, event | category | flops | bytes accessed | tf_op | source)
XLA Modules:
  0.0 386.7 jit_solution(8558500685093032469)
XLA Ops:
  6.5 1.6 fusion.67
  9.4 0.8 fusion.63
  10.1 1.0 select_reduce_fusion.1
  11.3 0.9 select_reduce_fusion.3
  12.6 42.3 %all-gather.2.cloned.1.call-done = bf16[1024,512]{1,0:T(8,128)(2,1)} async-done(((bf16[64,512]{1,0:T(8,128)(2,1)}), bf16[1024,512]{1,0:T(8,128)(2,1)}) %all-gather.2.cloned.1.call-update) | async-done | bytes 1048592 | tf_op jit(solution)/shard_map/all_gather | solution.py:95
  54.9 1.3 reshape.430
  56.2 0.7 gather_fusion
  59.1 0.8 fusion.70
  60.6 4.9 %all-to-all-start.2 = ((f32[16,1,256]{2,1,0:T(1,128)}), f32[16,1,256]{2,1,0:T(1,128)S(1)}, u32[]{:S(2)}, u32[]{:S(2)}) async-start(f32[16,1,256]{2,1,0:T(1,128)} %reshape.468), calls=%async_computation.2 | async-start | bytes 32768 | tf_op jit(solution)/shard_map/all_to_all | solution.py:115
  67.2 5.9 %all-to-all-done.2 = f32[16,1,256]{2,1,0:T(1,128)S(1)} async-done(((f32[16,1,256]{2,1,0:T(1,128)}), f32[16,1,256]{2,1,0:T(1,128)S(1)}, u32[]{:S(2)}, u32[]{:S(2)}) %all-to-all-start.2) | async-done | bytes 16416 | tf_op jit(solution)/shard_map/all_to_all | solution.py:115
  73.1 3.5 all-to-all-start.1
  76.6 2.4 convolution_bitcast_fusion
  79.0 5.1 %all-to-all-done.1 = f32[16,1,256]{2,1,0:T(1,128)S(1)} async-done(((f32[16,1,256]{2,1,0:T(1,128)}), f32[16,1,256]{2,1,0:T(1,128)S(1)}, u32[]{:S(2)}, u32[]{:S(2)}) %all-to-all-start.1) | async-done | bytes 16416 | tf_op jit(solution)/shard_map/all_to_all | solution.py:114
  84.2 3.7 all-to-all-start
  91.1 24.1 %all-to-all-done = f32[16,64,1,4,128]{4,1,3,2,0:T(8,128)S(1)} async-done(((f32[16,64,1,4,128]{4,1,3,2,0:T(8,128)}), f32[16,64,1,4,128]{4,1,3,2,0:T(8,128)S(1)}, u32[]{:S(2)}, u32[]{:S(2)}) %all-to-all-start) | async-done | bytes 2097184 | tf_op jit(solution)/shard_map/all_to_all | solution.py:116
  116.1 2.9 fusion.26
  119.1 1.3 copy-done.2
  122.2 60.5 %all-reduce.2.cloned.1.call-done = f32[128,4096]{1,0:T(8,128)} async-done(((f32[128,4096]{1,0:T(8,128)}), f32[128,4096]{1,0:T(8,128)}) %all-reduce.2.cloned.1.call-update) | async-done | bytes 2097168 | tf_op jit(solution)/shard_map/psum | solution.py:168
  182.7 2.0 multiply_reduce_fusion
  185.0 1.1 convolution_convert_fusion.1
  186.0 0.8 broadcast_in_dim.146
  186.8 79.0 %all_to_all.25 = bf16[16,48,4096]{2,1,0:T(8,128)(2,1)S(1)} all-to-all(bf16[16,48,4096]{2,1,0:T(8,128)(2,1)S(1)} %bitcast.149), channel_id=1, replica_groups=mesh['dp'=16,'mp'=8] {'dp'}, dimensions={0} | all-to-all | bytes 12582912 | tf_op jit(solution)/shard_map/all_to_all | solution.py:188
  265.8 7.5 %fusion.1 = f32[16,48,768]{2,1,0:T(8,128)S(1)} fusion(bf16[16,48,4096]{2,1,0:T(8,128)(2,1)S(1)} %all_to_all.25, bf16[4096,768]{1,0:T(8,128)(2,1)} %param.29), kind=kOutput, calls=%fused_computation.4 | convolution fusion | flops 4831838208 | bytes 14942208 | tf_op jit(solution)/shard_map/scd,df->scf/dot_general | solution.py:190
  273.3 5.3 %multiply_convert_fusion = bf16[16,48,768]{2,1,0:T(8,128)(2,1)S(1)} fusion(f32[16,48,768]{2,1,0:T(8,128)S(1)} %fusion.1, bf16[16,48,4096]{2,1,0:T(8,128)(2,1)S(1)} %all_to_all.25, bf16[4096,768]{1,0:T(8,128)(2,1)S(1)} %bitcast.157), kind=kOutput, calls=%fused_computation.9 | convolution fusion | flops 4835377152 | bytes 16121856 | tf_op jit(solution)/shard_map/scd,df->scf/dot_general | solution.py:189
  278.7 6.9 %convolution_convert_fusion = bf16[16,48,4096]{2,1,0:T(8,128)(2,1)} fusion(bf16[16,48,768]{2,1,0:T(8,128)(2,1)S(1)} %multiply_convert_fusion, bf16[768,4096]{1,0:T(8,128)(2,1)S(1)} %bitcast.159), kind=kOutput, calls=%fused_computation.2 | convolution fusion | flops 4834983936 | bytes 13762560 | tf_op jit(solution)/shard_map/scf,fd->scd/dot_general | solution.py:192
  285.6 41.4 %reduce-scatter.2.cloned.1.call-done = bf16[16,48,512]{2,1,0:T(8,128)(2,1)} async-done(((bf16[16,48,4096]{2,1,0:T(8,128)(2,1)}), bf16[16,48,512]{2,1,0:T(8,128)(2,1)}) %reduce-scatter.2.cloned.1.call-update) | async-done | bytes 786448 | tf_op jit(solution)/shard_map/reduce_scatter | solution.py:193
  327.0 2.5 convert_element_type.63
  329.5 7.0 %all-to-all-start.4 = ((f32[16,48,512]{2,1,0:T(8,128)}), f32[16,48,512]{2,1,0:T(8,128)}, u32[]{:S(2)}, u32[]{:S(2)}) async-start(f32[16,48,512]{2,1,0:T(8,128)} %convert_element_type.63), calls=%async_computation.5 | async-start | bytes 3145728 | tf_op jit(solution)/shard_map/all_to_all | solution.py:196
  336.7 23.3 %all-to-all-done.4 = f32[16,48,512]{2,1,0:T(8,128)} async-done(((f32[16,48,512]{2,1,0:T(8,128)}), f32[16,48,512]{2,1,0:T(8,128)}, u32[]{:S(2)}, u32[]{:S(2)}) %all-to-all-start.4) | async-done | bytes 1572896 | tf_op jit(solution)/shard_map/all_to_all | solution.py:196
  360.1 1.6 bitcast_reduce_fusion.1
  362.4 17.0 %psum.15 = f32[128]{0:T(128)S(1)} all-reduce(f32[128]{0:T(128)S(1)} %get-tuple-element.20), channel_id=1, replica_groups=mesh['dp'=16,'mp'=8] {'mp'}, use_global_device_ids=true, to_apply=%region_24.25 | all-reduce | flops 128 | bytes 1024 | tf_op jit(solution)/shard_map/psum | solution.py:204
  379.4 0.8 multiply_convert_fusion.3
  (109 shorter events, 13.2 us)
Async XLA Ops:
  6.5 59.0 %copy-start = (bf16[128,16,128]{2,1,0:T(8,128)(2,1)S(1)}, bf16[128,16,128]{2,1,0:T(8,128)(2,1)}, u32[]{:S(2)}) copy-start(bf16[128,16,128]{2,1,0:T(8,128)(2,1)} %param.21) | copy-start | bytes 1572868
  6.5 50.5 %copy-start.5 = (bf16[128,16,128]{2,1,0:T(8,128)(2,1)S(1)}, bf16[128,16,128]{2,1,0:T(8,128)(2,1)}, u32[]{:S(2)}) copy-start(bf16[128,16,128]{2,1,0:T(8,128)(2,1)} %param.20) | copy-start | bytes 1572868
  6.5 48.4 %all-gather.2.cloned.1.call-start = ((), (), s32[]{:S(2)}) async-start(), calls=%async_computation.6 | async-start | bytes 1114112 | tf_op jit(solution)/shard_map/all_gather | solution.py:95
  60.6 12.5 %all-to-all-start.2 = ((f32[16,1,256]{2,1,0:T(1,128)}), f32[16,1,256]{2,1,0:T(1,128)S(1)}, u32[]{:S(2)}, u32[]{:S(2)}) async-start(f32[16,1,256]{2,1,0:T(1,128)} %reshape.468), calls=%async_computation.2 | async-start | bytes 32768 | tf_op jit(solution)/shard_map/all_to_all | solution.py:115
  73.1 11.0 %all-to-all-start.1 = ((f32[16,1,256]{2,1,0:T(1,128)}), f32[16,1,256]{2,1,0:T(1,128)S(1)}, u32[]{:S(2)}, u32[]{:S(2)}) async-start(f32[16,1,256]{2,1,0:T(1,128)} %reshape.466), calls=%async_computation.1 | async-start | bytes 32768 | tf_op jit(solution)/shard_map/all_to_all | solution.py:114
  79.0 8.9 %copy-start.4 = (bf16[64,512]{1,0:T(8,128)(2,1)S(1)}, bf16[64,512]{1,0:T(8,128)(2,1)}, u32[]{:S(2)}) copy-start(bf16[64,512]{1,0:T(8,128)(2,1)} %get-tuple-element.12) | copy-start | bytes 196612
  79.0 9.0 %copy-start.7 = (bf16[128,128]{1,0:T(8,128)(2,1)S(1)}, bf16[128,128]{1,0:T(8,128)(2,1)}, u32[]{:S(2)}) copy-start(bf16[128,128]{1,0:T(8,128)(2,1)} %param.18) | copy-start | bytes 98308
  79.0 9.5 %copy-start.9 = (bf16[128,128]{1,0:T(8,128)(2,1)S(1)}, bf16[128,128]{1,0:T(8,128)(2,1)}, u32[]{:S(2)}) copy-start(bf16[128,128]{1,0:T(8,128)(2,1)} %param.19) | copy-start | bytes 98308
  84.2 31.0 %all-to-all-start = ((f32[16,64,1,4,128]{4,1,3,2,0:T(8,128)}), f32[16,64,1,4,128]{4,1,3,2,0:T(8,128)S(1)}, u32[]{:S(2)}, u32[]{:S(2)}) async-start(f32[16,64,1,4,128]{4,1,3,2,0:T(8,128)} %convolution_bitcast_fusion), calls=%async_computation | async-start | bytes 4194304 | tf_op jit(solution)/shard_map/all_to_all | solution.py:116
  87.9 94.8 %all-reduce.2.cloned.1.call-start = ((), (), s32[]{:S(2)}) async-start(), calls=%async_computation.7 | async-start | bytes 4194304 | tf_op jit(solution)/shard_map/psum | solution.py:168
  116.1 3.0 copy-start.6
  119.0 1.4 copy-start.10
  119.1 1.3 copy-start.2
  119.1 65.6 %copy-start.8 = (f32[4096]{0:T(1024)S(1)}, f32[4096]{0:T(1024)}, u32[]{:S(2)}) copy-start(f32[4096]{0:T(1024)} %param.25) | copy-start | bytes 49156
  120.4 206.6 %reduce-scatter.2.cloned.1.call-start = ((), (), s32[]{:S(2)}) async-start(), calls=%async_computation.8 | async-start | bytes 7077888 | tf_op jit(solution)/shard_map/reduce_scatter | solution.py:193
  182.7 2.2 copy-start.3
  186.8 86.5 %slice-start = ((s8[6291456]{0:T(1024)(128)(4,1)}), s8[4194304]{0:T(1024)(128)(4,1)S(1)}, s32[]{:S(2)}) async-start(s8[6291456]{0:T(1024)(128)(4,1)} %bitcast.156), calls=%async_computation.9 | async-start | bytes 8388608
  265.8 7.5 %slice-start.1 = ((s8[6291456]{0:T(1024)(128)(4,1)}), s8[2097152]{0:T(1024)(128)(4,1)S(1)}, s32[]{:S(2)}) async-start(s8[6291456]{0:T(1024)(128)(4,1)} %bitcast.156), calls=%async_computation.10 | async-start | bytes 4194304
  265.8 12.8 %slice-start.2 = ((s8[6291456]{0:T(1024)(128)(4,1)}), s8[4194304]{0:T(1024)(128)(4,1)S(1)}, s32[]{:S(2)}) async-start(s8[6291456]{0:T(1024)(128)(4,1)} %bitcast.158), calls=%async_computation.11 | async-start | bytes 8388608
  273.3 5.3 %slice-start.3 = ((s8[6291456]{0:T(1024)(128)(4,1)}), s8[2097152]{0:T(1024)(128)(4,1)S(1)}, s32[]{:S(2)}) async-start(s8[6291456]{0:T(1024)(128)(4,1)} %bitcast.158), calls=%async_computation.12 | async-start | bytes 4194304
  285.6 51.0 %copy-start.12 = (f32[128,2]{0,1:T(2,128)S(1)}, f32[128,2]{0,1:T(2,128)}, u32[]{:S(2)}) copy-start(f32[128,2]{0,1:T(2,128)} %param.27) | copy-start | bytes 3076
  329.5 30.5 %all-to-all-start.4 = ((f32[16,48,512]{2,1,0:T(8,128)}), f32[16,48,512]{2,1,0:T(8,128)}, u32[]{:S(2)}, u32[]{:S(2)}) async-start(f32[16,48,512]{2,1,0:T(8,128)} %convert_element_type.63), calls=%async_computation.5 | async-start | bytes 3145728 | tf_op jit(solution)/shard_map/all_to_all | solution.py:196
  336.6 42.8 %copy-start.11 = (f32[512]{0:T(512)S(1)}, f32[512]{0:T(512)}, u32[]{:S(2)}) copy-start(f32[512]{0:T(512)} %param.31) | copy-start | bytes 6148
  336.6 43.6 %copy-start.1 = (bf16[128,16,128]{2,1,0:T(8,128)(2,1)S(1)}, bf16[128,16,128]{2,1,0:T(8,128)(2,1)}, u32[]{:S(2)}) copy-start(bf16[128,16,128]{2,1,0:T(8,128)(2,1)} %param.21) | copy-start | bytes 1572868
Sparse Core Ops, SparseCore 0:
  9.5 45.3 all-gather.1
  120.5 62.1 all-reduce.1
  285.7 41.2 reduce-scatter.1
where the time goes:
time: 387 us
  waiting for transfers between devices  203 us (52%)
  blocking collectives  96 us (25%)
  matrix products  29.4 us (8%)
  starting transfers between devices  19.3 us (5%)
  other arithmetic  15.1 us (4%)
  between operations  13.6 us (4%)
  local copies, waits for them, and re-layouts  10.6 us (3%)
    all_to_all x1, blocking collectives, local(): lax.all_to_all(send, 'dp', split_axis=0, concat_axis=0, tiled=True)  79 us
    psum x1, waiting for transfers between devices, local(): hidden_full = lax.psum(head_terms, 'mp')  60.5 us
    all_gather x1, waiting for transfers between devices, local(): gathered = lax.all_gather(queries[:DEC], 'dp', axis=0, tiled=True)  42.3 us
    reduce_scatter x1, waiting for transfers between devices, local(): lax.psum_scatter(down_part.astype(jnp.bfloat16), 'mp', scatter_dimension=...  41.4 us
    all_to_all x1, waiting for transfers between devices, local(): lax.all_to_all(weighted, 'dp', split_axis=0, concat_axis=0, tiled=True)  24.1 us
    all_to_all x1, waiting for transfers between devices, local(): lax.all_to_all(shares, 'dp', split_axis=0, concat_axis=0, tiled=True)  23.3 us
    psum x1, blocking collectives, local(): square_last = lax.psum(jnp.sum(mixed * mixed, axis=1), 'mp')  17 us
  transfers between devices with their start and end apart: 7, of which 7 were waited for; matrix products, arithmetic and copies ran while one was open for 3% of the time, Pallas kernels for 0%

commit v1 on v0

--- a/solution.py
+++ b/solution.py
@@ -92,7 +92,11 @@
     pool_local = cache_keys.shape[0]
     request_total = cache_len.shape[0]
     query_heads = queries[:DEC].reshape(DEC, kv_local, group_size, HD)
-    gathered = lax.all_gather(queries[:DEC], "dp", axis=0, tiled=True)
+    part = queries[:DEC]
+    size = lax.axis_size("dp")
+    blocks = jnp.stack([part for _ in range(size)])
+    blocks = lax.all_to_all(blocks, "dp", split_axis=0, concat_axis=0)
+    gathered = jnp.concatenate(blocks, axis=0)
     gathered_heads = gathered.reshape(request_total, kv_local, group_size, HD)
     page_ids = dp_index * pool_local + lax.broadcasted_iota(jnp.int32, (pool_local,), 0)
     owners, key_ok = page_owner(page_ids, page_order, cache_len)

time: 387 us -> 365 us (0.943)
  waiting for transfers between devices: 203 us -> 177 us
  starting transfers between devices: 19.3 us -> 26.1 us
    all_gather x1 -> x0, waiting for transfers between devices: 42.3 us -> none  [local(): gathered = lax.all_gather(queries[:DEC], 'dp', axis=0, tiled=True)]
    all_to_all x0 -> x1, waiting for transfers between devices: none -> 15.9 us  [local(): blocks = lax.all_to_all(blocks, 'dp', split_axis=0, concat_axis=0)]
    all_to_all x0 -> x1, starting transfers between devices: none -> 8.26 us  [local(): blocks = lax.all_to_all(blocks, 'dp', split_axis=0, concat_axis=0)]
where the time goes in v1:
time: 365 us; the launch traced here: 364 us
  waiting for transfers between devices  177 us (48%)
  blocking collectives  96 us (26%)
  matrix products  29.4 us (8%)
  starting transfers between devices  26.1 us (7%)
  between operations  14 us (4%)
  other arithmetic  12.3 us (3%)
  local copies, waits for them, and re-layouts  9.97 us (3%)
    all_to_all x1, blocking collectives, local(): lax.all_to_all(send, 'dp', split_axis=0, concat_axis=0, tiled=True)  79 us
    psum x1, waiting for transfers between devices, local(): hidden_full = lax.psum(head_terms, 'mp')  60.5 us
    reduce_scatter x1, waiting for transfers between devices, local(): lax.psum_scatter(down_part.astype(jnp.bfloat16), 'mp', scatter_dimension=...  41.5 us
    all_to_all x1, waiting for transfers between devices, local(): lax.all_to_all(weighted, 'dp', split_axis=0, concat_axis=0, tiled=True)  24.2 us
    all_to_all x1, waiting for transfers between devices, local(): lax.all_to_all(shares, 'dp', split_axis=0, concat_axis=0, tiled=True)  23.3 us
    psum x1, blocking collectives, local(): square_last = lax.psum(jnp.sum(mixed * mixed, axis=1), 'mp')  17 us
    all_to_all x1, waiting for transfers between devices, local(): blocks = lax.all_to_all(blocks, 'dp', split_axis=0, concat_axis=0)  15.9 us
    all_to_all x1, starting transfers between devices, local(): blocks = lax.all_to_all(blocks, 'dp', split_axis=0, concat_axis=0)  8.26 us
  transfers between devices with their start and end apart: 7, of which 7 were waited for; matrix products, arithmetic and copies ran while one was open for 3% of the time, Pallas kernels for 0%

profile of v1, /device:TPU:0, one launch (start us, length us, event | category | flops | bytes accessed | tf_op | source)
XLA Modules:
  0.0 364.3 jit_solution(3078497446411939452)
XLA Ops:
  6.5 0.9 fusion.67
  7.5 1.1 stack.2
  8.6 8.3 %all-to-all-start = ((bf16[16,64,512]{2,1,0:T(8,128)(2,1)}), bf16[16,64,512]{2,1,0:T(8,128)(2,1)S(1)}, u32[]{:S(2)}, u32[]{:S(2)}) async-start(bf16[16,64,512]{2,1,0:T(8,128)(2,1)} %stack.2), calls=%async_computation | async-start | bytes 2097152 | tf_op jit(solution)/shard_map/all_to_all | solution.py:98
  18.6 15.9 %all-to-all-done = bf16[16,64,512]{2,1,0:T(8,128)(2,1)S(1)} async-done(((bf16[16,64,512]{2,1,0:T(8,128)(2,1)}), bf16[16,64,512]{2,1,0:T(8,128)(2,1)S(1)}, u32[]{:S(2)}, u32[]{:S(2)}) %all-to-all-start) | async-done | bytes 1048608 | tf_op jit(solution)/shard_map/all_to_all | solution.py:98
  34.8 0.7 gather_fusion
  37.6 0.8 fusion.70
  38.4 0.7 reshape.466
  39.1 3.5 all-to-all-start.3
  44.3 5.8 %all-to-all-done.3 = f32[16,1,256]{2,1,0:T(1,128)S(1)} async-done(((f32[16,1,256]{2,1,0:T(1,128)}), f32[16,1,256]{2,1,0:T(1,128)S(1)}, u32[]{:S(2)}, u32[]{:S(2)}) %all-to-all-start.3) | async-done | bytes 16416 | tf_op jit(solution)/shard_map/all_to_all | solution.py:119
  50.2 3.5 all-to-all-start.2
  53.7 2.4 convolution_bitcast_fusion
  56.1 5.1 %all-to-all-done.2 = f32[16,1,256]{2,1,0:T(1,128)S(1)} async-done(((f32[16,1,256]{2,1,0:T(1,128)}), f32[16,1,256]{2,1,0:T(1,128)S(1)}, u32[]{:S(2)}, u32[]{:S(2)}) %all-to-all-start.2) | async-done | bytes 16416 | tf_op jit(solution)/shard_map/all_to_all | solution.py:118
  61.2 3.7 %all-to-all-start.1 = ((f32[16,64,1,4,128]{4,1,3,2,0:T(8,128)}), f32[16,64,1,4,128]{4,1,3,2,0:T(8,128)S(1)}, u32[]{:S(2)}, u32[]{:S(2)}) async-start(f32[16,64,1,4,128]{4,1,3,2,0:T(8,128)} %convolution_bitcast_fusion), calls=%async_computation.1 | async-start | bytes 4194304 | tf_op jit(solution)/shard_map/all_to_all | solution.py:120
  68.2 24.2 %all-to-all-done.1 = f32[16,64,1,4,128]{4,1,3,2,0:T(8,128)S(1)} async-done(((f32[16,64,1,4,128]{4,1,3,2,0:T(8,128)}), f32[16,64,1,4,128]{4,1,3,2,0:T(8,128)S(1)}, u32[]{:S(2)}, u32[]{:S(2)}) %all-to-all-start.1) | async-done | bytes 2097184 | tf_op jit(solution)/shard_map/all_to_all | solution.py:120
  93.3 2.9 fusion.26
  96.3 1.3 copy-done.2
  99.4 60.5 %all-reduce.2.cloned.1.call-done = f32[128,4096]{1,0:T(8,128)} async-done(((f32[128,4096]{1,0:T(8,128)}), f32[128,4096]{1,0:T(8,128)}) %all-reduce.2.cloned.1.call-update) | async-done | bytes 2097168 | tf_op jit(solution)/shard_map/psum | solution.py:172
  159.9 2.0 multiply_reduce_fusion
  162.1 1.1 convolution_convert_fusion.1
  163.2 0.8 broadcast_in_dim.146
  164.0 79.0 %all_to_all.30 = bf16[16,48,4096]{2,1,0:T(8,128)(2,1)S(1)} all-to-all(bf16[16,48,4096]{2,1,0:T(8,128)(2,1)S(1)} %bitcast.149), channel_id=1, replica_groups=mesh['dp'=16,'mp'=8] {'dp'}, dimensions={0} | all-to-all | bytes 12582912 | tf_op jit(solution)/shard_map/all_to_all | solution.py:192
  243.0 7.5 %fusion.1 = f32[16,48,768]{2,1,0:T(8,128)S(1)} fusion(bf16[16,48,4096]{2,1,0:T(8,128)(2,1)S(1)} %all_to_all.30, bf16[4096,768]{1,0:T(8,128)(2,1)} %param.29), kind=kOutput, calls=%fused_computation.4 | convolution fusion | flops 4831838208 | bytes 14942208 | tf_op jit(solution)/shard_map/scd,df->scf/dot_general | solution.py:194
  250.5 5.3 %multiply_convert_fusion = bf16[16,48,768]{2,1,0:T(8,128)(2,1)S(1)} fusion(f32[16,48,768]{2,1,0:T(8,128)S(1)} %fusion.1, bf16[16,48,4096]{2,1,0:T(8,128)(2,1)S(1)} %all_to_all.30, bf16[4096,768]{1,0:T(8,128)(2,1)S(1)} %bitcast.157), kind=kOutput, calls=%fused_computation.9 | convolution fusion | flops 4835377152 | bytes 16121856 | tf_op jit(solution)/shard_map/scd,df->scf/dot_general | solution.py:193
  255.9 6.9 %convolution_convert_fusion = bf16[16,48,4096]{2,1,0:T(8,128)(2,1)} fusion(bf16[16,48,768]{2,1,0:T(8,128)(2,1)S(1)} %multiply_convert_fusion, bf16[768,4096]{1,0:T(8,128)(2,1)S(1)} %bitcast.159), kind=kOutput, calls=%fused_computation.2 | convolution fusion | flops 4834983936 | bytes 13762560 | tf_op jit(solution)/shard_map/scf,fd->scd/dot_general | solution.py:196
  262.8 41.5 %reduce-scatter.2.cloned.1.call-done = bf16[16,48,512]{2,1,0:T(8,128)(2,1)} async-done(((bf16[16,48,4096]{2,1,0:T(8,128)(2,1)}), bf16[16,48,512]{2,1,0:T(8,128)(2,1)}) %reduce-scatter.2.cloned.1.call-update) | async-done | bytes 786448 | tf_op jit(solution)/shard_map/reduce_scatter | solution.py:197
  304.3 2.5 convert_element_type.63
  306.8 7.0 %all-to-all-start.5 = ((f32[16,48,512]{2,1,0:T(8,128)}), f32[16,48,512]{2,1,0:T(8,128)}, u32[]{:S(2)}, u32[]{:S(2)}) async-start(f32[16,48,512]{2,1,0:T(8,128)} %convert_element_type.63), calls=%async_computation.6 | async-start | bytes 3145728 | tf_op jit(solution)/shard_map/all_to_all | solution.py:200
  314.0 23.3 %all-to-all-done.5 = f32[16,48,512]{2,1,0:T(8,128)} async-done(((f32[16,48,512]{2,1,0:T(8,128)}), f32[16,48,512]{2,1,0:T(8,128)}, u32[]{:S(2)}, u32[]{:S(2)}) %all-to-all-start.5) | async-done | bytes 1572896 | tf_op jit(solution)/shard_map/all_to_all | solution.py:200
  337.3 1.6 bitcast_reduce_fusion.1
  339.0 0.7 multiply_reduce_fusion.1
  339.7 17.0 %psum.15 = f32[128]{0:T(128)S(1)} all-reduce(f32[128]{0:T(128)S(1)} %get-tuple-element.20), channel_id=1, replica_groups=mesh['dp'=16,'mp'=8] {'mp'}, use_global_device_ids=true, to_apply=%region_24.25 | all-reduce | flops 128 | bytes 1024 | tf_op jit(solution)/shard_map/psum | solution.py:208
  356.7 0.8 multiply_convert_fusion.3
  (111 shorter events, 11.9 us)
Async XLA Ops:
  6.5 36.1 %copy-start = (bf16[128,16,128]{2,1,0:T(8,128)(2,1)S(1)}, bf16[128,16,128]{2,1,0:T(8,128)(2,1)}, u32[]{:S(2)}) copy-start(bf16[128,16,128]{2,1,0:T(8,128)(2,1)} %param.21) | copy-start | bytes 1572868
  6.5 10.3 %copy-start.6 = (s32[1024]{0:T(1024)S(1)}, s32[1024]{0:T(1024)}, u32[]{:S(2)}) copy-start(s32[1024]{0:T(1024)} %param.22) | copy-start | bytes 12292
  6.5 10.9 %copy-start.10 = (s32[2048]{0:T(1024)S(1)}, s32[2048]{0:T(1024)}, u32[]{:S(2)}) copy-start(s32[2048]{0:T(1024)} %param.23) | copy-start | bytes 24580
  8.6 26.9 %copy-start.4 = (bf16[128,16,128]{2,1,0:T(8,128)(2,1)S(1)}, bf16[128,16,128]{2,1,0:T(8,128)(2,1)}, u32[]{:S(2)}) copy-start(bf16[128,16,128]{2,1,0:T(8,128)(2,1)} %param.20) | copy-start | bytes 1572868
  8.6 25.9 %all-to-all-start = ((bf16[16,64,512]{2,1,0:T(8,128)(2,1)}), bf16[16,64,512]{2,1,0:T(8,128)(2,1)S(1)}, u32[]{:S(2)}, u32[]{:S(2)}) async-start(bf16[16,64,512]{2,1,0:T(8,128)(2,1)} %stack.2), calls=%async_computation | async-start | bytes 2097152 | tf_op jit(solution)/shard_map/all_to_all | solution.py:98
  39.1 11.0 %all-to-all-start.3 = ((f32[16,1,256]{2,1,0:T(1,128)}), f32[16,1,256]{2,1,0:T(1,128)S(1)}, u32[]{:S(2)}, u32[]{:S(2)}) async-start(f32[16,1,256]{2,1,0:T(1,128)} %reshape.466), calls=%async_computation.3 | async-start | bytes 32768 | tf_op jit(solution)/shard_map/all_to_all | solution.py:119
  50.2 11.0 %all-to-all-start.2 = ((f32[16,1,256]{2,1,0:T(1,128)}), f32[16,1,256]{2,1,0:T(1,128)S(1)}, u32[]{:S(2)}, u32[]{:S(2)}) async-start(f32[16,1,256]{2,1,0:T(1,128)} %reshape.464), calls=%async_computation.2 | async-start | bytes 32768 | tf_op jit(solution)/shard_map/all_to_all | solution.py:118
  56.1 8.9 %copy-start.7 = (bf16[128,128]{1,0:T(8,128)(2,1)S(1)}, bf16[128,128]{1,0:T(8,128)(2,1)}, u32[]{:S(2)}) copy-start(bf16[128,128]{1,0:T(8,128)(2,1)} %param.18) | copy-start | bytes 98308
  56.1 9.5 %copy-start.9 = (bf16[128,128]{1,0:T(8,128)(2,1)S(1)}, bf16[128,128]{1,0:T(8,128)(2,1)}, u32[]{:S(2)}) copy-start(bf16[128,128]{1,0:T(8,128)(2,1)} %param.19) | copy-start | bytes 98308
  61.2 31.2 %all-to-all-start.1 = ((f32[16,64,1,4,128]{4,1,3,2,0:T(8,128)}), f32[16,64,1,4,128]{4,1,3,2,0:T(8,128)S(1)}, u32[]{:S(2)}, u32[]{:S(2)}) async-start(f32[16,64,1,4,128]{4,1,3,2,0:T(8,128)} %convolution_bitcast_fusion), calls=%async_computation.1 | async-start | bytes 4194304 | tf_op jit(solution)/shard_map/all_to_all | solution.py:120
  64.9 95.0 %all-reduce.2.cloned.1.call-start = ((), (), s32[]{:S(2)}) async-start(), calls=%async_computation.7 | async-start | bytes 4194304 | tf_op jit(solution)/shard_map/psum | solution.py:172
  93.3 3.0 copy-start.5
  96.2 1.4 copy-start.11
  96.3 1.3 copy-start.2
  96.3 65.6 %copy-start.8 = (f32[4096]{0:T(1024)S(1)}, f32[4096]{0:T(1024)}, u32[]{:S(2)}) copy-start(f32[4096]{0:T(1024)} %param.25) | copy-start | bytes 49156
  97.6 206.7 %reduce-scatter.2.cloned.1.call-start = ((), (), s32[]{:S(2)}) async-start(), calls=%async_computation.8 | async-start | bytes 7077888 | tf_op jit(solution)/shard_map/reduce_scatter | solution.py:197
  159.9 2.2 copy-start.3
  164.0 86.5 %slice-start = ((s8[6291456]{0:T(1024)(128)(4,1)}), s8[4194304]{0:T(1024)(128)(4,1)S(1)}, s32[]{:S(2)}) async-start(s8[6291456]{0:T(1024)(128)(4,1)} %bitcast.156), calls=%async_computation.9 | async-start | bytes 8388608
  243.0 7.5 %slice-start.1 = ((s8[6291456]{0:T(1024)(128)(4,1)}), s8[2097152]{0:T(1024)(128)(4,1)S(1)}, s32[]{:S(2)}) async-start(s8[6291456]{0:T(1024)(128)(4,1)} %bitcast.156), calls=%async_computation.10 | async-start | bytes 4194304
  243.0 12.8 %slice-start.2 = ((s8[6291456]{0:T(1024)(128)(4,1)}), s8[4194304]{0:T(1024)(128)(4,1)S(1)}, s32[]{:S(2)}) async-start(s8[6291456]{0:T(1024)(128)(4,1)} %bitcast.158), calls=%async_computation.11 | async-start | bytes 8388608
  250.5 5.3 %slice-start.3 = ((s8[6291456]{0:T(1024)(128)(4,1)}), s8[2097152]{0:T(1024)(128)(4,1)S(1)}, s32[]{:S(2)}) async-start(s8[6291456]{0:T(1024)(128)(4,1)} %bitcast.158), calls=%async_computation.12 | async-start | bytes 4194304
  262.8 51.1 %copy-start.13 = (f32[128,2]{0,1:T(2,128)S(1)}, f32[128,2]{0,1:T(2,128)}, u32[]{:S(2)}) copy-start(f32[128,2]{0,1:T(2,128)} %param.27) | copy-start | bytes 3076
  306.8 30.5 %all-to-all-start.5 = ((f32[16,48,512]{2,1,0:T(8,128)}), f32[16,48,512]{2,1,0:T(8,128)}, u32[]{:S(2)}, u32[]{:S(2)}) async-start(f32[16,48,512]{2,1,0:T(8,128)} %convert_element_type.63), calls=%async_computation.6 | async-start | bytes 3145728 | tf_op jit(solution)/shard_map/all_to_all | solution.py:200
  313.9 42.8 %copy-start.12 = (f32[512]{0:T(512)S(1)}, f32[512]{0:T(512)}, u32[]{:S(2)}) copy-start(f32[512]{0:T(512)} %param.31) | copy-start | bytes 6148
  313.9 43.6 %copy-start.1 = (bf16[128,16,128]{2,1,0:T(8,128)(2,1)S(1)}, bf16[128,16,128]{2,1,0:T(8,128)(2,1)}, u32[]{:S(2)}) copy-start(bf16[128,16,128]{2,1,0:T(8,128)(2,1)} %param.21) | copy-start | bytes 1572868
Sparse Core Ops, SparseCore 0:
  97.7 62.1 all-reduce.1
  262.9 41.3 reduce-scatter.1
